TPU v7x, 32 devices: a whole 2x2x4 slice. The times are simulated.
32 devices in a mesh: dp: 16 (over z, y, x), tensor: 2 (over core).
Axes of the slice: x: 2, y: 2, z: 4, core: 2. Of those that a mesh axis runs over, the one named last changes fastest.
Arguments:
- tokens: bfloat16 [1024, 16, 2560], P('tensor', 'dp'), may hold values from -6 to 6
- pre_gain: float32 [2560], replicated, may hold values from 0.25 to 1.75
- z_weight: bfloat16 [2560, 5120], P(None, 'tensor'), may hold values from -0.125 to 0.125
- x_weight: bfloat16 [2560, 5120], P(None, 'tensor'), may hold values from -0.125 to 0.125
- bc_weight: bfloat16 [2560, 256], replicated, may hold values from -0.125 to 0.125
- dt_weight: bfloat16 [2560, 80], P(None, 'tensor'), may hold values from -0.125 to 0.125
- conv_x_weight: float32 [4, 5120], P(None, 'tensor'), may hold values from -3 to 3
- conv_x_bias: float32 [5120], P('tensor'), may hold values from -3 to 3
- conv_bc_weight: float32 [4, 256], replicated, may hold values from -3 to 3
- conv_bc_bias: float32 [256], replicated, may hold values from -3 to 3
- dt_bias: float32 [80], P('tensor'), may hold values from -4 to -2
- decay_log: float32 [80], P('tensor'), may hold values from -6 to 0
- skip_gain: float32 [80], P('tensor'), may hold values from 0.5 to 2
- norm_gain: float32 [5120], P('tensor'), may hold values from 0.25 to 1.75
- out_weight: bfloat16 [5120, 2560], P('tensor'), may hold values from -0.078125 to 0.078125
- cotangent: bfloat16 [1024, 16, 2560], P('tensor', 'dp'), may hold values from -6 to 6
Outputs:
- layer_out: bfloat16 [1024, 16, 2560], P('tensor', 'dp')
- grad_tokens: bfloat16 [1024, 16, 2560], P('tensor', 'dp')
- grad_pre_gain: float32 [2560], replicated
- grad_z_weight: float32 [2560, 5120], P('dp', 'tensor')
- grad_x_weight: float32 [2560, 5120], P('dp', 'tensor')
- grad_bc_weight: float32 [2560, 256], P('dp')
- grad_dt_weight: float32 [2560, 80], P('dp', 'tensor')
- grad_conv_x_weight: float32 [4, 5120], P(None, 'tensor')
- grad_conv_x_bias: float32 [5120], P('tensor')
- grad_conv_bc_weight: float32 [4, 256], replicated
- grad_conv_bc_bias: float32 [256], replicated
- grad_dt_bias: float32 [80], P('tensor')
- grad_decay_log: float32 [80], P('tensor')
- grad_skip_gain: float32 [80], P('tensor')
- grad_norm_gain: float32 [5120], P('tensor')
- grad_out_weight: float32 [5120, 2560], P('tensor', 'dp')
All inputs are finite; a program needn't handle non-finite values.
Results may differ from a plain program's by a relative error of at most 0.012.
The roundings to bfloat16 on the way count: a program that leaves them out, or rounds other values in their place, can miss the bound.
Values may be sent and summed in bfloat16 or wider, within the bound.
A program may use at most 384 MiB of HBM per device.

v0:
```python
import jax
import jax.numpy as jnp
from jax import lax
from jax.sharding import PartitionSpec as P

N = 128
Q = 256


EPSILON = 1e-05
PRECISE = lax.Precision.HIGHEST


def rms_scale(values):
    return lax.rsqrt(jnp.mean(values * values, axis=-1, keepdims=True) + EPSILON)


def causal_conv(series, kernel, offsets):
    taps = kernel.shape[0]
    length = series.shape[0]
    padding = [(taps - 1, 0)] + [(0, 0)] * (series.ndim - 1)
    padded = jnp.pad(series, padding)
    summed = offsets + kernel[0] * padded[0:length]
    for tap_index in range(1, taps):
        summed = summed + kernel[tap_index] * padded[tap_index : tap_index + length]
    return jax.nn.silu(summed)


def state_space(inputs, steps, rates, b_proj, c_proj):
    length, heads, width = inputs.shape
    blocks = length // Q
    x_blocks = inputs.reshape(blocks, Q, heads, width)
    dt_blocks = steps.reshape(blocks, Q, heads)
    b_blocks = b_proj.reshape(blocks, Q, -1)
    c_blocks = c_proj.reshape(blocks, Q, -1)
    cumulative = jnp.cumsum(dt_blocks * rates, axis=1)
    by_head = jnp.transpose(cumulative, (0, 2, 1))
    spread = by_head[:, :, :, None] - by_head[:, :, None, :]
    causal = jnp.arange(Q)[:, None] >= jnp.arange(Q)[None, :]
    decay = jnp.exp(jnp.where(causal, spread, -jnp.inf))
    scores = jnp.einsum("kin,kjn->kij", c_blocks, b_blocks, precision=PRECISE)
    mixing = decay * scores[:, None] * jnp.transpose(dt_blocks, (0, 2, 1))[:, :, None, :]
    within = jnp.einsum("khij,kjhp->kihp", mixing, x_blocks, precision=PRECISE)
    to_end = jnp.exp(cumulative[:, -1:, :] - cumulative) * dt_blocks
    weighted = x_blocks * to_end[..., None]
    states = jnp.einsum("kjhp,kjn->khpn", weighted, b_blocks, precision=PRECISE)
    block_decay = jnp.exp(cumulative[:, -1, :])

    def advance(carried, element):
        factor, fresh = element
        return (carried * factor[:, None, None] + fresh, carried)

    _, entering = lax.scan(advance, jnp.zeros_like(states[0]), (block_decay, states))
    across = (
        jnp.einsum("kin,khpn->kihp", c_blocks, entering, precision=PRECISE)
        * jnp.exp(cumulative)[..., None]
    )
    return (within + across).reshape(length, heads, width)


def mixer_part(
    gate_in, x_in, b_proj, c_proj, dt_raw, conv_weight, conv_bias, dt_bias, decay_log, skip_gain
):
    length = x_in.shape[0]
    heads = dt_bias.shape[0]
    conv_out = causal_conv(x_in, conv_weight, conv_bias).reshape(length, heads, -1)
    steps = jax.nn.softplus(dt_raw + dt_bias)
    result = (
        state_space(conv_out, steps, -jnp.exp(decay_log), b_proj, c_proj)
        + skip_gain[:, None] * conv_out
    )
    return result.reshape(length, -1) * jax.nn.silu(gate_in)


def mixer_batch(
    gate_in, x_in, b_proj, c_proj, dt_raw, conv_weight, conv_bias, dt_bias, decay_log, skip_gain
):
    mapped = jax.vmap(mixer_part, in_axes=(1, 1, 1, 1, 1, None, None, None, None, None), out_axes=1)
    return mapped(
        gate_in, x_in, b_proj, c_proj, dt_raw, conv_weight, conv_bias, dt_bias, decay_log, skip_gain
    )


def project(source, weight):
    return jnp.einsum("lsd,de->lse", source, weight, preferred_element_type=jnp.float32)


def back_project(grads, weight):
    return jnp.einsum("lse,de->lsd", grads, weight, preferred_element_type=jnp.float32)


def weight_grad(source, grads):
    return jnp.einsum("lsd,lse->de", source, grads, preferred_element_type=jnp.float32)


def body(
    tokens,
    pre_gain,
    z_weight,
    x_weight,
    bc_weight,
    dt_weight,
    conv_x_weight,
    conv_x_bias,
    conv_bc_weight,
    conv_bc_bias,
    dt_bias,
    decay_log,
    skip_gain,
    norm_gain,
    out_weight,
    cotangent,
):
    local_rows = tokens.shape[0]
    inner_total = z_weight.shape[1] * lax.axis_size("tensor")
    token_f = tokens.astype(jnp.float32)
    pre_scale = rms_scale(token_f)
    normed = (token_f * pre_scale * pre_gain).astype(jnp.bfloat16)
    gathered = lax.all_gather(normed, "tensor", axis=0, tiled=True)
    gate_in = project(gathered, z_weight)
    x_in = project(gathered, x_weight)
    bc_in = project(gathered, bc_weight)
    dt_raw = project(gathered, dt_weight)
    bc_conv, conv_back = jax.vjp(causal_conv, bc_in, conv_bc_weight, conv_bc_bias)
    mixed, mixer_back = jax.vjp(
        mixer_batch,
        gate_in,
        x_in,
        bc_conv[..., :N],
        bc_conv[..., N:],
        dt_raw,
        conv_x_weight,
        conv_x_bias,
        dt_bias,
        decay_log,
        skip_gain,
    )
    squares = lax.psum(jnp.sum(mixed * mixed, axis=-1), "tensor")
    gate_scale = lax.rsqrt(squares / inner_total + EPSILON)[..., None]
    gated = (mixed * gate_scale * norm_gain).astype(jnp.bfloat16)
    branch_out = lax.psum_scatter(
        jnp.einsum("lsc,cd->lsd", gated, out_weight, preferred_element_type=jnp.float32).astype(
            jnp.bfloat16
        ),
        "tensor",
        scatter_dimension=0,
        tiled=True,
    ).astype(jnp.float32)
    layer_out = (token_f + branch_out).astype(jnp.bfloat16)
    grad_all = lax.all_gather(cotangent, "tensor", axis=0, tiled=True)
    grad_out = jnp.einsum("lsc,lsd->cd", gated, grad_all, preferred_element_type=jnp.float32)
    d_gated = jnp.einsum("lsd,cd->lsc", grad_all, out_weight, preferred_element_type=jnp.float32)
    grad_norm = jnp.sum(d_gated * mixed * gate_scale, axis=(0, 1))
    scaled_grad = d_gated * norm_gain
    inner_dot = lax.psum(jnp.sum(scaled_grad * mixed, axis=-1), "tensor")[..., None]
    d_mixed = gate_scale * scaled_grad - mixed * gate_scale**3 * inner_dot / inner_total
    (
        grad_gate,
        grad_x,
        grad_b,
        grad_c,
        grad_dt,
        grad_conv_w,
        grad_conv_b,
        grad_dt_bias,
        grad_decay,
        grad_skip,
    ) = mixer_back(d_mixed)
    grad_bc_conv = lax.psum(jnp.concatenate([grad_b, grad_c], axis=-1), "tensor")
    grad_bc_in, grad_conv_bc_w, grad_conv_bc_b = conv_back(grad_bc_conv)
    low_gate = grad_gate.astype(jnp.bfloat16)
    low_x = grad_x.astype(jnp.bfloat16)
    low_bc = grad_bc_in.astype(jnp.bfloat16)
    low_dt = grad_dt.astype(jnp.bfloat16)
    grad_z = weight_grad(gathered, low_gate)
    grad_xw = weight_grad(gathered, low_x)
    grad_bcw = weight_grad(gathered, low_bc)
    grad_dtw = weight_grad(gathered, low_dt)
    summed = back_project(low_gate, z_weight) + back_project(low_x, x_weight)
    d_normed = lax.psum_scatter(
        summed + back_project(low_dt, dt_weight), "tensor", scatter_dimension=0, tiled=True
    )
    own_bc = lax.dynamic_slice_in_dim(low_bc, lax.axis_index("tensor") * local_rows, local_rows, 0)
    d_normed = d_normed + back_project(own_bc, bc_weight)
    grad_pre = lax.psum(jnp.sum(d_normed * token_f * pre_scale, axis=(0, 1)), ("dp", "tensor"))
    gained = d_normed * pre_gain
    grad_tokens = (
        cotangent.astype(jnp.float32)
        + pre_scale * gained
        - token_f * pre_scale**3 * jnp.mean(gained * token_f, axis=-1, keepdims=True)
    )
    (
        grad_norm,
        grad_conv_w,
        grad_conv_b,
        grad_conv_bc_w,
        grad_conv_bc_b,
        grad_dt_bias,
        grad_decay,
        grad_skip,
    ) = lax.psum(
        (
            grad_norm,
            grad_conv_w,
            grad_conv_b,
            grad_conv_bc_w,
            grad_conv_bc_b,
            grad_dt_bias,
            grad_decay,
            grad_skip,
        ),
        "dp",
    )
    grad_z, grad_xw, grad_bcw, grad_dtw, grad_out = (
        lax.psum_scatter(grad_z, "dp", scatter_dimension=0, tiled=True),
        lax.psum_scatter(grad_xw, "dp", scatter_dimension=0, tiled=True),
        lax.psum_scatter(grad_bcw, "dp", scatter_dimension=0, tiled=True),
        lax.psum_scatter(grad_dtw, "dp", scatter_dimension=0, tiled=True),
        lax.psum_scatter(grad_out, "dp", scatter_dimension=1, tiled=True),
    )
    return (
        layer_out,
        grad_tokens.astype(jnp.bfloat16),
        grad_pre,
        grad_z,
        grad_xw,
        grad_bcw,
        grad_dtw,
        grad_conv_w,
        grad_conv_b,
        grad_conv_bc_w,
        grad_conv_bc_b,
        grad_dt_bias,
        grad_decay,
        grad_skip,
        grad_norm,
        grad_out,
    )


def solution(mesh):
    in_specs = (
        P("tensor", "dp", None),
        P(),
        P(None, "tensor"),
        P(None, "tensor"),
        P(),
        P(None, "tensor"),
        P(None, "tensor"),
        P("tensor"),
        P(),
        P(),
        P("tensor"),
        P("tensor"),
        P("tensor"),
        P("tensor"),
        P("tensor", None),
        P("tensor", "dp", None),
    )
    out_specs = (
        P("tensor", "dp", None),
        P("tensor", "dp", None),
        P(),
        P("dp", "tensor"),
        P("dp", "tensor"),
        P("dp", None),
        P("dp", "tensor"),
        P(None, "tensor"),
        P("tensor"),
        P(),
        P(),
        P("tensor"),
        P("tensor"),
        P("tensor"),
        P("tensor"),
        P("tensor", "dp"),
    )
    return jax.shard_map(body, mesh=mesh, in_specs=in_specs, out_specs=out_specs, check_vma=False)
```

profile of v0, /device:TPU:10, one launch (start us, length us, event | category | flops | bytes accessed | tf_op | source)
XLA Modules:
  0.0 2692.8 jit_solution(12765737510297042214)
XLA Ops:
  7.3 2.5 fusion.51
  10.4 3.9 fusion.53
  16.2 14.9 all-gather.3.cloned.1.call-done
  31.1 4.8 compare_select_fusion.2
  36.2 2.5 reduce-window.14
  39.1 20.0 fusion.85
  59.1 10.5 fusion.38
  69.7 11.4 copy.182
  81.1 15.8 reshape.952
  101.5 4.0 fusion.81
  109.0 13.2 reshape.915
  122.2 6.2 broadcast_multiply_fusion
  128.5 10.9 fusion.101
  139.4 3.0 broadcast.257.clone
  142.4 13.1 while.34
  156.5 2.2 fusion.155
  158.7 10.9 fusion.69
  169.7 3.9 copy-done.4
  173.7 49.6 %bitcast_add_fusion.3 = f32[1,4,256,40,64]{2,4,3,1,0:T(8,128)} fusion(f32[4,256,40,64]{1,3,2,0:T(8,128)S(1)} %fusion.69, f32[4,256,40]{1,2,0:T(8,128)S(1)} %bitcast.329, f32[4,40,256]{2,1,0:T(8,128)S(1)} %copy-done.29, f32[4,256,256]{2,1,0:T(8,128)S(1)} %fusion.155, f32[4,40,256]{2,1,0:T(8,128)S(1)} %reduce_window_sum.50, ...), kind=kOutput, calls=%fused_computation.52 | convolution fusion | flops 8100249600 | bytes 33062912 | tf_op jit(solution)/shard_map/jvp(vmap(khij,kjhp->kihp))/dot_general | solution.py:43
  223.3 15.1 copy.229
  238.4 17.7 reshape.950
  256.1 27.1 %multiply_reduce_fusion.7 = (f32[1024]{0:T(1024)S(1)}, f32[1024,2560]{1,0:T(8,128)}, f32[1024,2560]{1,0:T(8,128)}) fusion(f32[1024,2560]{1,0:T(8,128)} %reshape.950, f32[1024,2560]{1,0:T(8,128)} %get-tuple-element.376, f32[2560]{0:T(1024)S(1)} %mul.719, bf16[2560,2560]{1,0:T(8,128)(2,1)} %param.22, bf16[1024,1,2560]{2,0,1:T(8,128)(2,1)} %all-gather.3.cloned.1.call-done), kind=kOutput, calls=%fused_computation.81 | convolution fusion | flops 13455850496 | bytes 60307456 | tf_op jit(solution)/shard_map/lsd,de->lse/dot_general | solution.py:85
  283.2 2.4 psum.84
  285.7 23.5 multiply_reduce_fusion.2
  309.2 2.4 psum.85
  311.6 24.3 multiply_reduce_fusion.3
  335.9 11.4 copy.198
  347.3 13.1 mul.745
  360.4 13.0 mul.749
  373.4 11.0 multiply_reduce_fusion.5
  384.4 22.6 fusion.104
  407.0 16.0 fusion.100
  423.0 15.8 copy.206
  438.8 69.4 %fusion.10 = (f32[4,40,256]{2,1,0:T(8,128)}, f32[4,40,256]{2,1,0:T(8,128)}, f32[4,40,256]{2,1,0:T(8,128)}, f32[4,256,256]{2,1,0:T(8,128)S(1)}) fusion(f32[4,40,256]{2,1,0:T(8,128)S(1)} %copy-done.30, f32[4,256,256]{2,1,0:T(8,128)} %copy-done.20, f32[4,40,256]{2,1,0:T(8,128)S(1)} %copy-done.32, pred[256,256]{1,0:T(8,128)(4,1)S(1)} %copy-done.45, ...), kind=kOutput, calls=%fused_computation.21 | convolution fusion | flops 8188993536 | bytes 23953408 | tf_op jit(solution)/shard_map/transpose(jvp(vmap(khij,kjhp->kihp)))/dot_general | solution.py:43
  511.3 3.0 broadcast.257
  514.2 16.2 while.35
  530.5 15.4 fusion.112
  545.9 13.1 fusion.29
  559.1 40.2 %bitcast_add_fusion.2 = f32[1,4,256,40,64]{2,4,3,1,0:T(8,128)} fusion(f32[4,40,64,256]{3,2,1,0:T(8,128)S(1)} %get-tuple-element.407, f32[4,256,40]{1,2,0:T(8,128)S(1)} %bitcast.337, f32[4,40,256]{2,1,0:T(8,128)S(1)} %copy-done.30, f32[4,256,256]{2,1,0:T(8,128)S(1)} %copy-done.21, f32[4,40,256]{2,1,0:T(8,128)S(1)} %copy-done.32, ...), kind=kOutput, calls=%fused_computation.51 | convolution fusion | flops 8100249600 | bytes 33062912 | tf_op jit(solution)/shard_map/transpose(jvp(vmap(khij,kjhp->kihp)))/dot_general | solution.py:43
  605.6 10.2 reduce-window.16
  616.4 2.3 fusion.131
  618.7 15.3 copy.230
  634.0 17.7 reshape.951
  651.7 25.6 fusion.32
  677.3 20.7 fusion.156
  698.1 15.7 multiply_bitcast_fusion.3
  714.6 5.1 fusion.71
  719.7 5.4 fusion.133
  725.1 17.5 fusion.50
  742.6 23.7 add_bitcast_fusion
  767.0 21.7 fusion.90
  790.8 2.7 multiply_reduce_fusion.10
  795.0 5.6 fusion.73
  800.6 24.0 fusion.64
  824.7 22.1 fusion.77
  847.1 22.2 fusion.75
  871.0 7.3 fusion.60
  878.3 41.2 %psum.87 = f32[2560]{0:T(1024)} all-reduce(f32[2560]{0:T(1024)S(1)} %get-tuple-element.316), channel_id=1, replica_groups=mesh['dp'=16,'tensor'=2] {'dp','tensor'}, use_global_device_ids=true, to_apply=%region_26.27 | all-reduce | flops 2560 | bytes 20480 | tf_op jit(solution)/shard_map/psum | solution.py:185
  919.5 7.4 fusion.57
  926.9 26.2 all-reduce.26.cloned.1.call-done
  953.1 77.7 %reduce-scatter.18.cloned.1.call-done = f32[160,256]{1,0:T(8,128)} async-done(((f32[2560,256]{1,0:T(8,128)}), f32[160,256]{1,0:T(8,128)}) %reduce-scatter.18.cloned.1.call-update) | async-done | bytes 163856 | tf_op jit(solution)/shard_map/reduce_scatter | solution.py:217
  1030.8 552.2 %reduce-scatter.20.cloned.1.call-done = f32[2560,160]{0,1:T(8,128)} async-done(((f32[2560,2560]{0,1:T(8,128)}), f32[2560,160]{0,1:T(8,128)}) %reduce-scatter.20.cloned.1.call-update) | async-done | bytes 1638416 | tf_op jit(solution)/shard_map/reduce_scatter | solution.py:219
  1583.1 546.4 %reduce-scatter.14.cloned.1.call-done = f32[160,2560]{1,0:T(8,128)} async-done(((f32[2560,2560]{1,0:T(8,128)}), f32[160,2560]{1,0:T(8,128)}) %reduce-scatter.14.cloned.1.call-update) | async-done | bytes 1638416 | tf_op jit(solution)/shard_map/reduce_scatter | solution.py:215
  2129.5 546.6 %reduce-scatter.16.cloned.1.call-done = f32[160,2560]{1,0:T(8,128)} async-done(((f32[2560,2560]{1,0:T(8,128)}), f32[160,2560]{1,0:T(8,128)}) %reduce-scatter.16.cloned.1.call-update) | async-done | bytes 1638416 | tf_op jit(solution)/shard_map/reduce_scatter | solution.py:216
  (305 shorter events, 67.9 us)
Async XLA Ops:
  7.2 94.4 %copy-start = (bf16[2560,256]{1,0:T(8,128)(2,1)S(1)}, bf16[2560,256]{1,0:T(8,128)(2,1)}, u32[]{:S(2)}) copy-start(bf16[2560,256]{1,0:T(8,128)(2,1)} %param.24) | copy-start | bytes 3932164
  7.2 23.8 copy-start.22
  7.3 23.8 copy-start.71
  7.3 23.8 all-gather.3.cloned.1.call-start
  14.3 271.4 %all-gather.5.cloned.1.call-start = ((), (), s32[]{:S(2)}) async-start(), calls=%async_computation.9 | async-start | bytes 7864320 | tf_op jit(solution)/shard_map/all_gather | solution.py:150
  15.1 775.7 %all-reduce.24.cloned.1.call-start = ((), (), s32[]{:S(2)}) async-start(), calls=%async_computation.11 | async-start | bytes 2097152 | tf_op jit(solution)/shard_map/psum | solution.py:169
  15.8 20.4 copy-start.72
  15.8 89.7 %copy-start.61 = (f32[1,256]{1,0:T(1,128)}, f32[1,256]{1,0:T(1,128)S(1)}, u32[]{:S(2)}) copy-start(f32[1,256]{1,0:T(1,128)S(1)} %get-tuple-element.396) | copy-start | bytes 3076
  15.8 89.7 %copy-start.63 = (f32[1,256]{1,0:T(1,128)}, f32[1,256]{1,0:T(1,128)S(1)}, u32[]{:S(2)}) copy-start(f32[1,256]{1,0:T(1,128)S(1)} %get-tuple-element.397) | copy-start | bytes 3076
  15.9 89.7 %copy-start.65 = (f32[1,256]{1,0:T(1,128)}, f32[1,256]{1,0:T(1,128)S(1)}, u32[]{:S(2)}) copy-start(f32[1,256]{1,0:T(1,128)S(1)} %get-tuple-element.398) | copy-start | bytes 3076
  15.9 89.7 %copy-start.67 = (f32[1,256]{1,0:T(1,128)}, f32[1,256]{1,0:T(1,128)S(1)}, u32[]{:S(2)}) copy-start(f32[1,256]{1,0:T(1,128)S(1)} %get-tuple-element.399) | copy-start | bytes 3076
  16.0 295.6 %copy-start.41 = (f32[2560]{0:T(1024)}, f32[2560]{0:T(1024)S(1)}, u32[]{:S(2)}) copy-start(f32[2560]{0:T(1024)S(1)} %mul.719) | copy-start | bytes 30724
  16.1 42.9 %copy-start.33 = (f32[2560]{0:T(1024)}, f32[2560]{0:T(1024)S(1)}, u32[]{:S(2)}) copy-start(f32[2560]{0:T(1024)S(1)} %get-tuple-element.325) | copy-start | bytes 30724
  16.1 42.9 %copy-start.35 = (f32[2560]{0:T(1024)}, f32[2560]{0:T(1024)S(1)}, u32[]{:S(2)}) copy-start(f32[2560]{0:T(1024)S(1)} %get-tuple-element.326) | copy-start | bytes 30724
  16.2 42.9 %copy-start.37 = (f32[2560]{0:T(1024)}, f32[2560]{0:T(1024)S(1)}, u32[]{:S(2)}) copy-start(f32[2560]{0:T(1024)S(1)} %get-tuple-element.327) | copy-start | bytes 30724
  16.2 42.9 %copy-start.39 = (f32[2560]{0:T(1024)}, f32[2560]{0:T(1024)S(1)}, u32[]{:S(2)}) copy-start(f32[2560]{0:T(1024)S(1)} %get-tuple-element.328) | copy-start | bytes 30724
  36.0 64.9 %copy-start.12 = (f32[1,4,256,40]{2,1,3,0:T(4,128)}, f32[1,4,256,40]{2,1,3,0:T(4,128)S(1)}, u32[]{:S(2)}) copy-start(f32[1,4,256,40]{2,1,3,0:T(4,128)S(1)} %reshape.916) | copy-start | bytes 491524
  39.1 20.0 copy-start.58
  99.9 69.7 %copy-start.18 = (f32[1,4,256,40]{2,3,0,1:T(8,128)}, f32[1,4,256,40]{2,3,0,1:T(8,128)S(1)}, u32[]{:S(2)}) copy-start(f32[1,4,256,40]{2,3,0,1:T(8,128)S(1)} %copy.282) | copy-start | bytes 491524
  109.0 49.7 %copy-start.7 = (f32[1024,1,128]{2,0,1:T(8,128)}, f32[1024,1,128]{2,0,1:T(8,128)S(1)}, u32[]{:S(2)}) copy-start(f32[1024,1,128]{2,0,1:T(8,128)S(1)} %get-tuple-element.393) | copy-start | bytes 1572868
  156.5 17.2 slice-start.2
  158.7 14.9 slice-start.3
  256.1 29.6 %copy-start.59 = (f32[2560]{0:T(1024)S(1)}, f32[2560]{0:T(1024)}, u32[]{:S(2)}) copy-start(f32[2560]{0:T(1024)} %param.33) | copy-start | bytes 30724
  285.6 26.0 copy-start.52
  384.4 22.6 copy-start.8
  423.0 15.8 copy-start.30
  423.0 15.8 copy-start.32
  423.0 15.8 copy-start.45
  438.8 71.4 %copy-start.10 = (f32[1024,1,128]{2,0,1:T(8,128)S(1)}, f32[1024,1,128]{2,0,1:T(8,128)}, u32[]{:S(2)}) copy-start(f32[1024,1,128]{2,0,1:T(8,128)} %get-tuple-element.392) | copy-start | bytes 1572868
  438.8 71.4 %copy-start.17 = (f32[4,256,128]{2,1,0:T(8,128)S(1)}, f32[4,256,128]{2,1,0:T(8,128)}, u32[]{:S(2)}) copy-start(f32[4,256,128]{2,1,0:T(8,128)} %fusion.104) | copy-start | bytes 1572868
  438.8 75.4 %copy-start.2 = (f32[1,40,64,128]{3,2,1,0:T(8,128)S(1)}, f32[1,40,64,128]{3,2,1,0:T(8,128)}, u32[]{:S(2)}) copy-start(f32[1,40,64,128]{3,2,1,0:T(8,128)} %custom-call.1) | copy-start | bytes 3932164
  530.4 15.4 slice-start
  530.5 15.4 copy-start.11
  530.5 15.4 slice-start.1
  559.0 43.5 %copy-start.15 = (f32[1,4,256,40]{2,0,3,1:T(1,128)S(1)}, f32[1,4,256,40]{2,0,3,1:T(1,128)}, u32[]{:S(2)}) copy-start(f32[1,4,256,40]{2,0,3,1:T(1,128)} %copy-done.14) | copy-start | bytes 491524
  559.0 43.8 %copy-start.13 = (f32[1,4,256,40]{2,1,3,0:T(4,128)S(1)}, f32[1,4,256,40]{2,1,3,0:T(4,128)}, u32[]{:S(2)}) copy-start(f32[1,4,256,40]{2,1,3,0:T(4,128)} %copy-done.12) | copy-start | bytes 491524
  559.0 43.8 %copy-start.55 = (f32[4,40]{1,0:T(4,128)S(1)}, f32[4,40]{1,0:T(4,128)}, u32[]{:S(2)}) copy-start(f32[4,40]{1,0:T(4,128)} %copy-done.54) | copy-start | bytes 1924
  559.0 46.0 %copy-start.24 = (f32[4,256,40]{1,2,0:T(8,128)S(1)}, f32[4,256,40]{1,2,0:T(8,128)}, u32[]{:S(2)}) copy-start(f32[4,256,40]{1,2,0:T(8,128)} %multiply_reduce_fusion.5) | copy-start | bytes 491524
  559.1 57.3 %copy-start.73 = (f32[40]{0:T(128)S(1)}, f32[40]{0:T(128)}, u32[]{:S(2)}) copy-start(f32[40]{0:T(128)} %copy-done.72) | copy-start | bytes 484
  602.4 267.0 %reduce-scatter.22.cloned.1.call-start = ((), (), s32[]{:S(2)}) async-start(), calls=%async_computation.16 | async-start | bytes 1392640
  634.0 17.7 copy-start.42
  677.3 20.7 copy-start.34
  677.3 20.7 copy-start.36
  677.3 20.7 copy-start.38
  677.3 20.7 copy-start.40
  698.1 15.7 copy-start.25
  698.1 21.6 copy-start.23
  725.1 145.9 %reduce-scatter.12.cloned.1.call-start = ((), (), s32[]{:S(2)}) async-start(), calls=%async_computation.10 | async-start | bytes 15728640 | tf_op jit(solution)/shard_map/reduce_scatter | solution.py:180
  766.3 22.5 copy-start.46
  766.3 22.5 copy-start.50
  766.4 22.5 copy-start.49
  766.4 22.5 copy-start.48
  766.4 22.6 copy-start.47
  766.4 23.2 copy-start.75
  766.4 23.2 copy-start.78
  766.4 24.4 copy-start.6
  766.4 24.4 copy-start.16
  766.4 153.0 %reduce-scatter.10.cloned.1.call-start = ((), (), s32[]{:S(2)}) async-start(), calls=%async_computation.8 | async-start | bytes 7864320 | tf_op jit(solution)/shard_map/reduce_scatter | solution.py:141
  788.7 164.4 %all-reduce.26.cloned.1.call-start = ((), (), s32[]{:S(2)}) async-start(), calls=%async_computation.17 | async-start | bytes 144384 | tf_op jit(solution)/shard_map/psum | solution.py:201
  794.8 236.0 %reduce-scatter.18.cloned.1.call-start = ((), (), s32[]{:S(2)}) async-start(), calls=%async_computation.14 | async-start | bytes 2785280 | tf_op jit(solution)/shard_map/reduce_scatter | solution.py:217
  800.6 782.5 %reduce-scatter.20.cloned.1.call-start = ((), (), s32[]{:S(2)}) async-start(), calls=%async_computation.15 | async-start | bytes 27852800 | tf_op jit(solution)/shard_map/reduce_scatter | solution.py:219
  824.6 1304.8 %reduce-scatter.14.cloned.1.call-start = ((), (), s32[]{:S(2)}) async-start(), calls=%async_computation.12 | async-start | bytes 27852800 | tf_op jit(solution)/shard_map/reduce_scatter | solution.py:215
  846.8 1829.2 %reduce-scatter.16.cloned.1.call-start = ((), (), s32[]{:S(2)}) async-start(), calls=%async_computation.13 | async-start | bytes 27852800 | tf_op jit(solution)/shard_map/reduce_scatter | solution.py:216
  869.4 50.1 %copy-start.69 = (f32[512]{0:T(512)S(1)}, f32[512]{0:T(512)}, u32[]{:S(2)}) copy-start(f32[512]{0:T(512)} %get-tuple-element.400) | copy-start | bytes 6148
  (31 other events, 239.8 us)
Sparse Core Ops, SparseCore 0:
  14.4 16.6 all-gather.2
  32.6 16.3 all-gather.4
  602.5 20.7 all-reduce.23
  725.2 68.7 reduce-scatter.21
  796.3 26.4 reduce-scatter.11
  825.0 14.4 reduce-scatter.9
  847.1 105.9 all-reduce.25
  955.9 74.8 reduce-scatter.17
  1033.7 549.3 reduce-scatter.19
  1585.8 543.6 reduce-scatter.13
  2132.4 543.6 reduce-scatter.15
where the time goes:
time: 2700 us; the launch traced here: 2690 us
  waiting for transfers between devices  1760 us (65%)
  matrix products  490 us (18%)
  local copies, waits for them, and re-layouts  195 us (7%)
  other arithmetic  180 us (7%)
  blocking collectives  46.1 us (2%)
    reduce_scatter x1, waiting for transfers between devices, body(): lax.psum_scatter(grad_out, 'dp', scatter_dimension=1, tiled=True)  552 us
    reduce_scatter x1, waiting for transfers between devices, body(): lax.psum_scatter(grad_xw, 'dp', scatter_dimension=0, tiled=True)  547 us
    reduce_scatter x1, waiting for transfers between devices, body(): lax.psum_scatter(grad_z, 'dp', scatter_dimension=0, tiled=True)  546 us
    dot_general x3, matrix products, state_space(): within = jnp.einsum('khij,kjhp->kihp', mixing, x_blocks, precision=PRECISE)  159 us
    reduce_scatter x1, waiting for transfers between devices, body(): lax.psum_scatter(grad_bcw, 'dp', scatter_dimension=0, tiled=True)  77.7 us
    reshape x4, local copies, waits for them, and re-layouts, state_space(): x_blocks = inputs.reshape(blocks, Q, heads, width)  64.5 us
    dot_general x4, matrix products, back_project(): jnp.einsum('lse,de->lsd', grads, weight, preferred_element_type=jnp.float32)  57.1 us
    dot_general x4, matrix products, project(): jnp.einsum('lsd,de->lse', source, weight, preferred_element_type=jnp.floa...  55.8 us
  transfers between devices with their start and end apart: 11, of which 6 were waited for; matrix products, arithmetic and copies ran while one was open for 20% of the time, Pallas kernels for 0%

commit v1 on v0

v1 whole, which is shorter than its diff:
```python
import jax
import jax.numpy as jnp
import numpy as np
from jax import lax
from jax.sharding import PartitionSpec as P

N = 128
Q = 256


EPSILON = 1e-05
PRECISE = lax.Precision.HIGHEST
BOTH = ("dp", "tensor")
F32 = jnp.float32
BF16 = jnp.bfloat16


def causal_conv(series, kernel, offsets):
    taps = kernel.shape[0]
    length = series.shape[0]
    padding = [(taps - 1, 0)] + [(0, 0)] * (series.ndim - 1)
    padded = jnp.pad(series, padding)
    summed = offsets + kernel[0] * padded[0:length]
    for tap_index in range(1, taps):
        summed = summed + kernel[tap_index] * padded[tap_index : tap_index + length]
    return jax.nn.silu(summed)


def state_space(inputs, steps, rates, b_proj, c_proj):
    length, heads, width = inputs.shape
    blocks = length // Q
    x_blocks = inputs.reshape(blocks, Q, heads, width)
    dt_blocks = steps.reshape(blocks, Q, heads)
    b_blocks = b_proj.reshape(blocks, Q, -1)
    c_blocks = c_proj.reshape(blocks, Q, -1)
    cumulative = jnp.cumsum(dt_blocks * rates, axis=1)
    by_head = jnp.transpose(cumulative, (0, 2, 1))
    spread = by_head[:, :, :, None] - by_head[:, :, None, :]
    causal = jnp.arange(Q)[:, None] >= jnp.arange(Q)[None, :]
    decay = jnp.exp(jnp.where(causal, spread, -jnp.inf))
    scores = jnp.einsum("kin,kjn->kij", c_blocks, b_blocks, precision=PRECISE)
    mixing = decay * scores[:, None] * jnp.transpose(dt_blocks, (0, 2, 1))[:, :, None, :]
    within = jnp.einsum("khij,kjhp->kihp", mixing, x_blocks, precision=PRECISE)
    to_end = jnp.exp(cumulative[:, -1:, :] - cumulative) * dt_blocks
    weighted = x_blocks * to_end[..., None]
    states = jnp.einsum("kjhp,kjn->khpn", weighted, b_blocks, precision=PRECISE)
    block_decay = jnp.exp(cumulative[:, -1, :])

    def advance(carried, element):
        factor, fresh = element
        return (carried * factor[:, None, None] + fresh, carried)

    _, entering = lax.scan(advance, jnp.zeros_like(states[0]), (block_decay, states))
    across = (
        jnp.einsum("kin,khpn->kihp", c_blocks, entering, precision=PRECISE)
        * jnp.exp(cumulative)[..., None]
    )
    return (within + across).reshape(length, heads, width)


def scan_part(x_in, b_proj, c_proj, dt_raw, conv_weight, conv_bias, dt_bias, decay_log, skip_gain):
    length = x_in.shape[0]
    heads = dt_bias.shape[0]
    conv_out = causal_conv(x_in, conv_weight, conv_bias).reshape(length, heads, -1)
    steps = jax.nn.softplus(dt_raw + dt_bias)
    result = (
        state_space(conv_out, steps, -jnp.exp(decay_log), b_proj, c_proj)
        + skip_gain[:, None] * conv_out
    )
    return result.reshape(length, -1)


def mm(a, b, dims, out=F32):
    return lax.dot_general(a, b, (dims, ((), ())), preferred_element_type=out)


def bit_orders(count):
    bits = count.bit_length() - 1
    rest = list(range(bits - 1, 1, -1))
    return [0, 1][:bits] + rest, [1, 0][-bits:] + rest if bits > 1 else [0]


def solution(mesh):
    count = mesh.shape["dp"]
    orders = bit_orders(count)
    levels = len(orders[0])
    tables = np.zeros((2, count), np.int32)
    for side in range(2):
        for place in range(count):
            tables[side, place] = sum(
                ((place >> (levels - 1 - k)) & 1) << orders[side][k] for k in range(levels)
            )
    swaps = []
    for k in range(levels):
        swaps.append(
            [
                (d * 2 + t, (d ^ (1 << orders[t][k])) * 2 + t)
                for d in range(count)
                for t in range(2)
            ]
        )
    flip = [(0, 1), (1, 0)]

    def other(value):
        return lax.ppermute(value, "tensor", flip)

    def pair_sum(value):
        return value + other(value)

    def level(k, values):
        half = values.shape[0] // 2
        came = lax.ppermute(values[half:].astype(BF16), BOTH, swaps[k])
        return values[:half] + came.astype(F32)

    def scatter_product(left, right):
        half = left.shape[0] // 2
        send = mm(left[half:], right, ((1,), (0,)), BF16)
        came = lax.ppermute(send, BOTH, swaps[0])
        keep = lax.optimization_barrier(mm(left[:half], right, ((1,), (0,))))
        total = keep + came.astype(F32)
        for k in range(1, levels):
            total = level(k, total)
        return total

    def body(
        tokens,
        pre_gain,
        z_weight,
        x_weight,
        bc_weight,
        dt_weight,
        conv_x_weight,
        conv_x_bias,
        conv_bc_weight,
        conv_bc_bias,
        dt_bias,
        decay_log,
        skip_gain,
        norm_gain,
        out_weight,
        cotangent,
    ):
        rows, _, width = tokens.shape
        inner_total = z_weight.shape[1] * 2
        me = lax.axis_index("dp")
        side = lax.axis_index("tensor")
        own_tokens = tokens[:, 0]
        own_grad = cotangent[:, 0]
        far_tokens = other(own_tokens)
        far_grad = other(own_grad)

        def join(own, far):
            return jnp.where(
                side == 0, jnp.concatenate([own, far], 0), jnp.concatenate([far, own], 0)
            )

        def own_half(value):
            return lax.dynamic_slice_in_dim(value, side * rows, rows, 0)

        def far_half(value):
            return lax.dynamic_slice_in_dim(value, (1 - side) * rows, rows, 0)

        grad_all = join(own_grad, far_grad)
        token_all = join(own_tokens, far_tokens).astype(F32)
        scale_all = lax.rsqrt(jnp.mean(token_all * token_all, axis=-1, keepdims=True) + EPSILON)
        normed = (token_all * scale_all * pre_gain).astype(BF16)

        places = jnp.where(side == 0, jnp.asarray(tables[0]), jnp.asarray(tables[1])) ^ me

        def travel_order(value):
            turned = lax.optimization_barrier(value.T).reshape(count, width // count, -1)
            return turned[places].reshape(width, -1)

        normed_turned = travel_order(normed)
        grad_turned = travel_order(grad_all)

        gate_in = mm(normed, z_weight, ((1,), (0,)))
        x_in = mm(normed, x_weight, ((1,), (0,)))
        bc_in = mm(normed, bc_weight, ((1,), (0,)))
        dt_raw = mm(normed, dt_weight, ((1,), (0,)))
        bc_conv, conv_back = jax.vjp(causal_conv, bc_in, conv_bc_weight, conv_bc_bias)
        y, scan_back = jax.vjp(
            scan_part,
            x_in,
            bc_conv[:, :N],
            bc_conv[:, N:],
            dt_raw,
            conv_x_weight,
            conv_x_bias,
            dt_bias,
            decay_log,
            skip_gain,
        )
        sig = jax.nn.sigmoid(gate_in)
        mixed = y * gate_in * sig
        squares = pair_sum(jnp.sum(mixed * mixed, axis=-1, keepdims=True))
        gate_scale = lax.rsqrt(squares / inner_total + EPSILON)
        gated = (mixed * gate_scale * norm_gain).astype(BF16)
        grad_out = scatter_product(grad_turned, gated).T

        d_gated = mm(grad_all, out_weight, ((1,), (1,)))
        grad_norm = jnp.sum(d_gated * mixed * gate_scale, axis=0)
        scaled = d_gated * norm_gain
        inner_dot = pair_sum(jnp.sum(scaled * mixed, axis=-1, keepdims=True))
        d_mixed = gate_scale * scaled - mixed * gate_scale**3 * inner_dot / inner_total
        low_gate = (d_mixed * y * sig * (1.0 + gate_in * (1.0 - sig))).astype(BF16)
        grad_z = scatter_product(normed_turned, low_gate)

        far_branch = other(mm(far_half(gated), out_weight, ((1,), (0,)), BF16))
        own_branch = mm(own_half(gated), out_weight, ((1,), (0,)))
        token_f = own_tokens.astype(F32)
        layer_out = (token_f + own_branch + far_branch.astype(F32)).astype(BF16)

        (
            grad_x_in,
            grad_b,
            grad_c,
            grad_dt,
            grad_conv_w,
            grad_conv_b,
            grad_dt_bias,
            grad_decay,
            grad_skip,
        ) = scan_back(d_mixed * gate_in * sig)
        low_x = grad_x_in.astype(BF16)
        grad_xw = scatter_product(normed_turned, low_x)
        grad_bc_conv = pair_sum(jnp.concatenate([grad_b, grad_c], axis=-1))
        grad_bc_in, grad_conv_bc_w, grad_conv_bc_b = conv_back(grad_bc_conv)
        low_bc = grad_bc_in.astype(BF16)
        low_dt = grad_dt.astype(BF16)
        half_bc = lax.dynamic_slice_in_dim(low_bc, side * N, N, 1)
        grad_small = scatter_product(
            normed_turned,
            jnp.concatenate([half_bc, low_dt], axis=-1),
        )
        own_bcw = grad_small[:, :N]
        far_bcw = other(own_bcw)
        grad_bcw = jnp.where(
            side == 0,
            jnp.concatenate([own_bcw, far_bcw], 1),
            jnp.concatenate([far_bcw, own_bcw], 1),
        )
        grad_dtw = grad_small[:, N:]

        def back(part):
            return (
                mm(part(low_gate), z_weight, ((1,), (1,)))
                + mm(part(low_x), x_weight, ((1,), (1,)))
                + mm(part(low_dt), dt_weight, ((1,), (1,)))
            )

        far_back = other(back(far_half))
        d_normed = back(own_half) + mm(own_half(low_bc), bc_weight, ((1,), (1,))) + far_back
        pre_scale = own_half(scale_all)
        grad_pre = lax.psum(jnp.sum(d_normed * token_f * pre_scale, axis=0), BOTH)
        gained = d_normed * pre_gain
        grad_tokens = (
            own_grad.astype(F32)
            + pre_scale * gained
            - token_f * pre_scale**3 * jnp.mean(gained * token_f, axis=-1, keepdims=True)
        )
        (
            grad_norm,
            grad_conv_w,
            grad_conv_b,
            grad_conv_bc_w,
            grad_conv_bc_b,
            grad_dt_bias,
            grad_decay,
            grad_skip,
        ) = lax.psum(
            (
                grad_norm,
                grad_conv_w,
                grad_conv_b,
                grad_conv_bc_w,
                grad_conv_bc_b,
                grad_dt_bias,
                grad_decay,
                grad_skip,
            ),
            "dp",
        )
        return (
            layer_out[:, None],
            grad_tokens.astype(BF16)[:, None],
            grad_pre,
            grad_z,
            grad_xw,
            grad_bcw,
            grad_dtw,
            grad_conv_w,
            grad_conv_b,
            grad_conv_bc_w,
            grad_conv_bc_b,
            grad_dt_bias,
            grad_decay,
            grad_skip,
            grad_norm,
            grad_out,
        )

    in_specs = (
        P("tensor", "dp", None),
        P(),
        P(None, "tensor"),
        P(None, "tensor"),
        P(),
        P(None, "tensor"),
        P(None, "tensor"),
        P("tensor"),
        P(),
        P(),
        P("tensor"),
        P("tensor"),
        P("tensor"),
        P("tensor"),
        P("tensor", None),
        P("tensor", "dp", None),
    )
    out_specs = (
        P("tensor", "dp", None),
        P("tensor", "dp", None),
        P(),
        P("dp", "tensor"),
        P("dp", "tensor"),
        P("dp", None),
        P("dp", "tensor"),
        P(None, "tensor"),
        P("tensor"),
        P(),
        P(),
        P("tensor"),
        P("tensor"),
        P("tensor"),
        P("tensor"),
        P("tensor", "dp"),
    )
    return jax.shard_map(body, mesh=mesh, in_specs=in_specs, out_specs=out_specs, check_vma=False)
```

time: 2700 us -> 1390 us (0.51)
  waiting for transfers between devices: 1760 us -> 328 us
  other arithmetic: 180 us -> 232 us
  blocking collectives: 46.1 us -> 76.7 us
  starting transfers between devices: 0.84 us -> 29.4 us
    reduce_scatter x6 -> x0, waiting for transfers between devices: 1720 us -> none  [the longest x1 552 us: body(): lax.psum_scatter(grad_out, 'dp', scatter_dimension=1, tiled=True)]
    ppermute x0 -> x24, waiting for transfers between devices: none -> 328 us  [the longest x12 232 us: level(): came = lax.ppermute(values[half:].astype(BF16), BOTH, swaps[k])]
    add x0 -> x16, other arithmetic: none -> 58.1 us  [the longest x4 33 us: scatter_product(): total = keep + came.astype(F32)]
    mul x8 -> x3, local copies, waits for them, and re-layouts: 49.8 us -> 12.2 us  [the longest x1 11.4 us: body(): d_mixed * gate_in * sig]
    psum x3 -> x1, blocking collectives: 46.1 us -> 76.7 us  [body(): grad_pre = lax.psum(jnp.sum(d_normed * token_f * pre_scale, axis=0), BOTH)]
    ppermute x0 -> x24, starting transfers between devices: none -> 29.4 us  [the longest x12 23.4 us: level(): came = lax.ppermute(values[half:].astype(BF16), BOTH, swaps[k])]
    slice x3 -> x19, local copies, waits for them, and re-layouts: 1.06 us -> 29.7 us  [the longest x12 17.5 us: level(): came = lax.ppermute(values[half:].astype(BF16), BOTH, swaps[k])]
    dot_general x14 -> x22, matrix products: 232 us -> 233 us  [mm(): return lax.dot_general(a, b, (dims, ((), ())), preferred_element_type=out)]
  transfers between devices with their start and end apart: 11 -> 25, of which waited for: 6 -> 13; matrix products, arithmetic and copies ran while one was open for 20% -> 33% of each run, Pallas kernels for 0% -> 0%
where the time goes in v1:
time: 1390 us; the launch traced here: 1380 us
  matrix products  484 us (35%)
  waiting for transfers between devices  328 us (24%)
  other arithmetic  232 us (17%)
  local copies, waits for them, and re-layouts  212 us (15%)
  blocking collectives  76.7 us (6%)
  starting transfers between devices  29.4 us (2%)
  between operations  15.7 us (1%)
    dot_general x22, matrix products, mm(): return lax.dot_general(a, b, (dims, ((), ())), preferred_element_type=out)  233 us
    ppermute x12, waiting for transfers between devices, level(): came = lax.ppermute(values[half:].astype(BF16), BOTH, swaps[k])  232 us
    dot_general x3, matrix products, state_space(): within = jnp.einsum('khij,kjhp->kihp', mixing, x_blocks, precision=PRECISE)  155 us
    ppermute x4, waiting for transfers between devices, scatter_product(): came = lax.ppermute(send, BOTH, swaps[0])  96.6 us
    psum x1, blocking collectives, body(): grad_pre = lax.psum(jnp.sum(d_normed * token_f * pre_scale, axis=0), BOTH)  76.7 us
    reshape x4, local copies, waits for them, and re-layouts, state_space(): x_blocks = inputs.reshape(blocks, Q, heads, width)  64.3 us
    dot_general x3, matrix products, state_space(): jnp.einsum('kin,khpn->kihp', c_blocks, entering, precision=PRECISE)  46.9 us
    dot_general x3, matrix products, state_space(): states = jnp.einsum('kjhp,kjn->khpn', weighted, b_blocks, precision=PRECISE)  45.9 us
  transfers between devices with their start and end apart: 25, of which 13 were waited for; matrix products, arithmetic and copies ran while one was open for 33% of the time, Pallas kernels for 0%

profile of v1, /device:TPU:10, one launch (start us, length us, event | category | flops | bytes accessed | tf_op | source)
XLA Modules:
  0.0 1378.8 jit_solution(2713497785616016151)
XLA Ops:
  13.3 5.9 fusion.23
  33.3 18.3 %fusion.127 = f32[1024,2560]{1,0:T(8,128)S(1)} fusion(bf16[1024,2560]{1,0:T(8,128)(2,1)} %copy-done.6, bf16[2560,2560]{1,0:T(8,128)(2,1)} %param.25), kind=kOutput, calls=%fused_computation.256 | convolution fusion | flops 13421772800 | bytes 28835840 | tf_op jit(solution)/shard_map/dot_general | solution.py:74
  51.8 10.5 fusion.29
  62.3 15.7 %reshape.298 = f32[4,256,40,64]{3,2,1,0:T(8,128)} reshape(f32[1024,2560]{1,0:T(8,128)} %get-tuple-element.386) | data formatting | bytes 20971520 | tf_op jit(solution)/shard_map/jvp()/reshape;jvp()/reshape | solution.py:32
  77.9 15.9 %copy.169 = f32[4,256,40,64]{1,3,2,0:T(8,128)} copy(f32[4,256,40,64]{3,2,1,0:T(8,128)} %reshape.298) | data formatting | bytes 20971520 | tf_op jit(solution)/shard_map/jvp()/reshape;jvp()/reshape | solution.py:32
  99.8 10.8 fusion.35
  113.7 13.1 while.34
  126.8 11.3 fusion.130
  142.5 50.2 %bitcast_add_fusion.3 = f32[4,256,40,64]{1,3,2,0:T(8,128)} fusion(f32[4,256,40,64]{1,3,2,0:T(8,128)S(1)} %fusion.130, f32[4,256,40]{1,2,0:T(8,128)S(1)} %get-tuple-element.412, f32[4,256,40,64]{1,3,2,0:T(8,128)} %copy.169, f32[4,40,256]{2,1,0:T(8,128)S(1)} %copy.168, f32[4,256,256]{2,1,0:T(8,128)S(1)} %fusion.129, f32[4,40,256]{2,1,0:T(8,128)S(1)} %copy-done.52, ...), kind=kOutput, calls=%fused_computation.51 | convolution fusion | flops 8100249600 | bytes 33062912 | tf_op jit(solution)/shard_map/jvp(khij,kjhp->kihp)/dot_general | solution.py:43
  192.6 15.1 %copy.202 = f32[4,256,40,64]{3,2,1,0:T(8,128)} copy(f32[4,256,40,64]{1,3,2,0:T(8,128)} %bitcast_add_fusion.3) | data formatting | bytes 20971520 | tf_op jit(solution)/shard_map/jvp()/reshape | solution.py:58
  207.7 17.7 %reshape.296 = f32[1024,2560]{1,0:T(8,128)} reshape(f32[4,256,40,64]{3,2,1,0:T(8,128)} %copy.202) | data formatting | bytes 20971520 | tf_op jit(solution)/shard_map/jvp()/reshape | solution.py:58
  225.4 27.6 %multiply_reduce_fusion.11 = (f32[1024]{0:T(1024)S(1)}, f32[1024,2560]{1,0:T(8,128)}, f32[1024,2560]{1,0:T(8,128)}) fusion(f32[1024,2560]{1,0:T(8,128)} %reshape.296, f32[1024,2560]{1,0:T(8,128)} %get-tuple-element.387, f32[2560]{0:T(1024)S(1)} %mul.590, bf16[1024,2560]{1,0:T(8,128)(2,1)} %copy-done.6, bf16[2560,2560]{1,0:T(8,128)(2,1)} %param.24), kind=kOutput, calls=%fused_computation.65 | convolution fusion | flops 13455850496 | bytes 60307456 | tf_op jit(solution)/shard_map/dot_general | solution.py:74
  253.1 6.9 fusion.77
  260.0 8.1 copy.195
  268.1 5.9 gather_fusion.1
  279.6 7.9 copy.192
  287.6 5.8 gather_fusion
  293.4 5.7 fusion.124
  299.2 24.9 %multiply_reduce_fusion.2 = (f32[2560]{0:T(1024)}, f32[1024]{0:T(1024)S(1)}, f32[1024,2560]{1,0:T(8,128)}) fusion(f32[1024,2560]{1,0:T(8,128)} %get-tuple-element.385, f32[1024]{0:T(1024)S(1)} %bitcast.325, f32[2560]{0:T(1024)S(1)} %copy-done.79, bf16[2560,2560]{1,0:T(8,128)(2,1)} %param.36, bf16[512,2560]{1,0:T(8,128)(2,1)} %collective-permute-done.3, ...), kind=kOutput, calls=%fused_computation.52 | convolution fusion | flops 13461091328 | bytes 39350272 | tf_op jit(solution)/shard_map/dot_general | solution.py:74
  325.4 26.4 %multiply_reduce_fusion.3 = (f32[2560]{0:T(1024)}, f32[1024,2560]{1,0:T(8,128)}, bf16[1024,2560]{1,0:T(8,128)(2,1)}, bf16[1024,2560]{1,0:T(8,128)(2,1)}) fusion(f32[1024,2560]{1,0:T(8,128)} %get-tuple-element.387, f32[1024,2560]{1,0:T(8,128)} %get-tuple-element.420, f32[1024]{0:T(1024)S(1)} %bitcast.323, f32[1024,2560]{1,0:T(8,128)} %get-tuple-element.385, ...), kind=kLoop, calls=%fused_computation.53 | loop fusion | flops 76019200 | bytes 73443328 | tf_op jit(solution)/shard_map/transpose(jvp())/reduce_sum | solution.py:68
  351.8 11.4 copy.174
  363.1 13.1 reshape.256
  376.2 16.0 %fusion.38 = f32[4,40,64,128]{3,2,1,0:T(8,128)} fusion(f32[4,256,128,1]{2,1,3,0:T(8,128)S(1)} %bitcast.284, f32[4,256,40,64]{1,0,3,2:T(4,128)} %reshape.256, f32[4,256,40]{1,2,0:T(8,128)S(1)} %copy-done.43), kind=kOutput, calls=%fused_computation.83 | convolution fusion | flops 4029153280 | bytes 16416768 | tf_op jit(solution)/shard_map/transpose(jvp(kin,khpn->kihp))/dot_general | solution.py:55
  392.2 19.7 %fusion.69 = f32[4,256,128]{2,1,0:T(8,128)} fusion(f32[4,40,64,128]{3,2,1,0:T(8,128)} %get-tuple-element.541, f32[4,256,40,64]{1,0,3,2:T(4,128)S(1)} %copy-done.2, f32[4,256,40]{1,2,0:T(8,128)S(1)} %copy-done.43), kind=kOutput, calls=%fused_computation.141 | convolution fusion | flops 4029153280 | bytes 16416768 | tf_op jit(solution)/shard_map/transpose(jvp(kin,khpn->kihp))/dot_general | solution.py:55
  414.9 15.7 %while.35 = (s32[]{:T(128)}, f32[40,64,128]{2,1,0:T(8,128)S(1)}, f32[4,40]{1,0:T(4,128)S(1)}, f32[4,40,64,128]{3,2,1,0:T(8,128)}, f32[4,40,64,128]{3,2,1,0:T(8,1...) while((s32[]{:T(128)}, f32[40,64,128]{2,1,0:T(8,128)S(1)}, ...), condition=%wide.region_9.10_spmd.clone, body=%wide.region_7.9_spmd.clone.sunk | while | flops 1966044 | bytes 7865420 | solution.py:53
  430.6 21.6 %fusion.70 = f32[4,256,128]{2,1,0:T(8,128)} fusion(f32[4,40,64,128]{3,2,1,0:T(8,128)} %get-tuple-element.193, f32[4,256,40,64]{1,3,2,0:T(8,128)} %copy.169, f32[4,256,40]{1,2,0:T(8,128)S(1)} %copy-done.38), kind=kOutput, calls=%fused_computation.142 | convolution fusion | flops 4029153280 | bytes 16416768 | tf_op jit(solution)/shard_map/transpose(jvp(kjhp,kjn->khpn))/dot_general | solution.py:46
  452.2 13.5 multiply_reduce_fusion.9
  465.7 11.2 multiply_reduce_fusion.8
  477.0 66.4 %fusion.10 = (f32[4,40,256]{2,1,0:T(8,128)}, f32[4,40,256]{2,1,0:T(8,128)}, f32[4,40,256]{2,1,0:T(8,128)}, f32[4,256,256]{2,1,0:T(8,128)}) fusion(f32[4,40,256]{2,1,0:T(8,128)} %copy-done.54, f32[4,256,256]{2,1,0:T(8,128)} %copy-done.44, f32[4,40,256]{2,1,0:T(8,128)} %get-tuple-element.410, pred[256,256]{1,0:T(8,128)(4,1)S(1)} %copy-done.71, ...), kind=kOutput, calls=%fused_computation.22 | convolution fusion | flops 8188993536 | bytes 23953408 | tf_op jit(solution)/shard_map/transpose(jvp(khij,kjhp->kihp))/dot_general | solution.py:43
  543.4 38.2 %bitcast_add_fusion.2 = f32[4,256,40,64]{1,3,2,0:T(8,128)} fusion(f32[4,256,40,64]{1,3,2,0:T(8,128)S(1)} %copy-done.17, f32[4,256,40]{1,2,0:T(8,128)S(1)} %copy-done.39, f32[4,40,256]{2,1,0:T(8,128)S(1)} %copy-done.55, f32[4,256,256]{2,1,0:T(8,128)S(1)} %copy-done.45, f32[4,40,256]{2,1,0:T(8,128)S(1)} %copy-done.53, pred[256,256]{1,0:T(8,128)(4,1)S(1)} %copy-done.71, ...), kind=kOutput, calls=%fused_computation.50 | convolution fusion | flops 8100249600 | bytes 33062912 | tf_op jit(solution)/shard_map/transpose(jvp(khij,kjhp->kihp))/dot_general | solution.py:43
  581.6 15.1 %copy.203 = f32[4,256,40,64]{3,2,1,0:T(8,128)} copy(f32[4,256,40,64]{1,3,2,0:T(8,128)} %bitcast_add_fusion.2) | data formatting | bytes 20971520 | tf_op jit(solution)/shard_map/transpose(jvp())/reshape | solution.py:32
  596.7 17.7 %reshape.297 = f32[1024,2560]{1,0:T(8,128)} reshape(f32[4,256,40,64]{3,2,1,0:T(8,128)} %copy.203) | data formatting | bytes 20971520 | tf_op jit(solution)/shard_map/transpose(jvp())/reshape | solution.py:32
  614.4 25.3 %multiply_reduce_fusion.7 = (f32[2560]{0:T(1024)S(1)}, f32[2560]{0:T(1024)S(1)}, f32[2560]{0:T(1024)S(1)}, f32[2560]{0:T(1024)S(1)}, f32[2560]{0:T(1024)}, /*index=5*/f32[1024,2560]{1,0:T(8,128)S(1)}) fusion(f32[1024,2560]{1,0:T(8,128)} %copy-done.7, f32[1024,2560]{1,0:T(8,128)} %get-tuple-element.387, f32[1024,2560]{1,0:T(8,128)} %reshape.297, ...), kind=kLoop, calls=%fused_computation.57 | loop fusion | flops 52416000 | bytes 52490240 | tf_op jit(solution)/shard_map/transpose(jvp())/reduce_sum | solution.py:25
  639.8 15.1 %broadcast_multiply_fusion = (f32[1024,2560]{1,0:T(8,128)}, f32[1024,2560]{1,0:T(8,128)}, f32[1024,2560]{1,0:T(8,128)}, f32[1024,2560]{1,0:T(8,128)}) fusion(f32[1024,2560]{1,0:T(8,128)S(1)} %get-tuple-element.381, f32[2560]{0:T(1024)S(1)} %copy-done.63, f32[2560]{0:T(1024)S(1)} %copy-done.59, f32[2560]{0:T(1024)S(1)} %copy-done.61, f32[2560]{0:T(1024)S(1)} %copy-done.65), kind=kLoop, calls=%fused_computation.110 | loop fusion | flops 10485760 | bytes 52469760 | tf_op jit(solution)/shard_map/transpose(jvp())/mul | solution.py:25
  654.9 15.2 %fusion.28 = bf16[1024,2560]{1,0:T(8,128)(2,1)S(1)} fusion(f32[1024,2560]{1,0:T(8,128)} %get-tuple-element.395, f32[1024,2560]{1,0:T(8,128)} %get-tuple-element.396, f32[1024,2560]{1,0:T(8,128)} %get-tuple-element.397, f32[1024,2560]{1,0:T(8,128)} %get-tuple-element.394), kind=kLoop, calls=%fused_computation.47 | loop fusion | flops 10485760 | bytes 47185920 | tf_op jit(solution)/shard_map/convert.13
  670.2 9.4 fusion.134
  679.6 10.0 fusion.133
  689.6 9.0 fusion.132
  698.6 9.9 fusion.131
  709.3 10.2 reduce-window.16
  720.9 12.5 fusion.59
  736.7 11.7 fusion.62
  751.6 9.0 fusion.136
  761.2 10.2 fusion.135
  776.3 11.0 fusion.65
  793.2 16.5 %add_add_fusion = f32[512,2560]{1,0:T(8,128)} fusion(f32[512,2560]{1,0:T(8,128)} %fusion.94, f32[512,2560]{1,0:T(8,128)} %fusion.59, bf16[2560,2560]{1,0:T(8,128)(2,1)} %param.24, bf16[1024,2560]{1,0:T(8,128)(2,1)} %get-tuple-element.392, s32[]{:T(128)S(6)} %select_n.74), kind=kOutput, calls=%fused_computation.104 | convolution fusion | flops 6713507840 | bytes 31457284 | tf_op jit(solution)/shard_map/dot_general | solution.py:74
  812.9 96.5 %collective-permute-done.15 = bf16[1280,168]{0,1:T(8,128)(2,1)S(1)} collective-permute-done((bf16[1280,168]{0,1:T(8,128)(2,1)S(1)}, bf16[1280,168]{0,1:T(8,128)(2,1)S(1)}, u32[]{:S(2)}, u32[]{:S(2)}) %collective-permute-start.15) | collective-permute-done | bytes 430112 | tf_op jit(solution)/shard_map/ppermute | solution.py:118
  930.0 14.6 %fusion.55 = bf16[512,1,2560]{2,0,1:T(8,128)(2,1)} fusion(bf16[512,2560]{1,0:T(8,128)(2,1)} %collective-permute-done.2, bf16[2560,2560]{1,0:T(8,128)(2,1)} %param.36, bf16[1024,2560]{1,0:T(8,128)(2,1)} %get-tuple-element.393, s32[]{:T(128)S(6)} %select_n.73, bf16[512,1,2560]{2,0,1:T(8,128)(2,1)} %param.22), kind=kOutput, calls=%fused_computation.114 | convolution fusion | flops 6717440000 | bytes 23592964 | tf_op jit(solution)/shard_map/dot_general | solution.py:74
  944.7 18.1 %fusion.46 = (f32[2560]{0:T(1024)S(1)}, f32[512]{0:T(512)S(1)}, f32[512,2560]{1,0:T(8,128)}) fusion(f32[512]{0:T(512)S(1)} %copy-done.77, bf16[512,1,2560]{2,0,1:T(8,128)(2,1)} %param.22, f32[2560]{0:T(1024)S(1)} %copy-done.73, f32[512,2560]{1,0:T(8,128)} %collective-permute-done.6, f32[512,2560]{1,0:T(8,128)} %fusion.81, f32[512,2560]{1,0:T(8,128)} %fusion.96, ...), kind=kOutput, calls=%fused_computation.101 | convolution fusion | flops 6725301248 | bytes 44589060 | tf_op jit(solution)/shard_map/dot_general | solution.py:74
  962.7 76.7 %psum.63 = f32[2560]{0:T(1024)} all-reduce(f32[2560]{0:T(1024)S(1)} %get-tuple-element.331), channel_id=1, replica_groups=mesh['dp'=16,'tensor'=2] {'dp','tensor'}, use_global_device_ids=true, to_apply=%region_21.22 | all-reduce | flops 2560 | bytes 20480 | tf_op jit(solution)/shard_map/psum | solution.py:255
  1039.4 7.5 convert_add_fusion
  1048.3 12.7 convert_add_fusion.1
  1067.2 12.7 convert_add_fusion.2
  1089.0 5.9 slice_add_fusion
  1098.4 22.9 %collective-permute-done.12 = bf16[640,2560]{1,0:T(8,128)(2,1)} collective-permute-done((bf16[640,2560]{1,0:T(8,128)(2,1)}, bf16[640,2560]{1,0:T(8,128)(2,1)}, u32[]{:S(2)}, u32[]{:S(2)}) %collective-permute-start.12) | collective-permute-done | bytes 3276832 | tf_op jit(solution)/shard_map/ppermute | solution.py:112
  1121.3 7.5 slice_add_fusion.1
  1132.3 24.1 %collective-permute-done.8 = bf16[640,2560]{1,0:T(8,128)(2,1)} collective-permute-done((bf16[640,2560]{1,0:T(8,128)(2,1)}, bf16[640,2560]{1,0:T(8,128)(2,1)}, u32[]{:S(2)}, u32[]{:S(2)}) %collective-permute-start.8) | collective-permute-done | bytes 3276832 | tf_op jit(solution)/shard_map/ppermute | solution.py:112
  1156.4 5.7 slice_add_fusion.2
  1165.9 71.0 %collective-permute-done.22 = bf16[320,2560]{1,0:T(8,128)(2,1)S(1)} collective-permute-done((bf16[320,2560]{1,0:T(8,128)(2,1)S(1)}, bf16[320,2560]{1,0:T(8,128)(2,1)S(1)}, u32[]{:S(2)}, u32[]{:S(2)}) %collective-permute-start.22) | collective-permute-done | bytes 1638432 | tf_op jit(solution)/shard_map/ppermute | solution.py:112
  1242.8 29.2 %collective-permute-done.13 = bf16[320,2560]{1,0:T(8,128)(2,1)S(1)} collective-permute-done((bf16[320,2560]{1,0:T(8,128)(2,1)S(1)}, bf16[320,2560]{1,0:T(8,128)(2,1)S(1)}, u32[]{:S(2)}, u32[]{:S(2)}) %collective-permute-start.13) | collective-permute-done | bytes 1638432 | tf_op jit(solution)/shard_map/ppermute | solution.py:112
  1275.9 30.9 %collective-permute-done.9 = bf16[320,2560]{1,0:T(8,128)(2,1)S(1)} collective-permute-done((bf16[320,2560]{1,0:T(8,128)(2,1)S(1)}, bf16[320,2560]{1,0:T(8,128)(2,1)S(1)}, u32[]{:S(2)}, u32[]{:S(2)}) %collective-permute-start.9) | collective-permute-done | bytes 1638432 | tf_op jit(solution)/shard_map/ppermute | solution.py:112
  1310.9 14.5 %collective-permute-done.23 = bf16[160,2560]{1,0:T(8,128)(2,1)S(1)} collective-permute-done((bf16[160,2560]{1,0:T(8,128)(2,1)S(1)}, bf16[160,2560]{1,0:T(8,128)(2,1)S(1)}, u32[]{:S(2)}, u32[]{:S(2)}) %collective-permute-start.23) | collective-permute-done | bytes 819232 | tf_op jit(solution)/shard_map/ppermute | solution.py:112
  1326.7 16.2 %collective-permute-done.14 = bf16[160,2560]{1,0:T(8,128)(2,1)S(1)} collective-permute-done((bf16[160,2560]{1,0:T(8,128)(2,1)S(1)}, bf16[160,2560]{1,0:T(8,128)(2,1)S(1)}, u32[]{:S(2)}, u32[]{:S(2)}) %collective-permute-start.14) | collective-permute-done | bytes 819232 | tf_op jit(solution)/shard_map/ppermute | solution.py:112
  1344.3 16.1 %collective-permute-done.10 = bf16[160,2560]{1,0:T(8,128)(2,1)S(1)} collective-permute-done((bf16[160,2560]{1,0:T(8,128)(2,1)S(1)}, bf16[160,2560]{1,0:T(8,128)(2,1)S(1)}, u32[]{:S(2)}, u32[]{:S(2)}) %collective-permute-start.10) | collective-permute-done | bytes 819232 | tf_op jit(solution)/shard_map/ppermute | solution.py:112
  (421 shorter events, 171.0 us)
Async XLA Ops:
  7.2 86.6 %copy-start = (bf16[2560,256]{1,0:T(8,128)(2,1)S(1)}, bf16[2560,256]{1,0:T(8,128)(2,1)}, u32[]{:S(2)}) copy-start(bf16[2560,256]{1,0:T(8,128)(2,1)} %param.26) | copy-start | bytes 3932164
  7.2 1354.6 %all-reduce.23.cloned.1.call-start = ((), (), s32[]{:S(2)}) async-start(), calls=%async_computation | async-start | bytes 144384 | tf_op jit(solution)/shard_map/psum | solution.py:271
  7.2 6.1 collective-permute-start
  7.3 245.8 %collective-permute-start.3 = (bf16[512,2560]{1,0:T(8,128)(2,1)}, bf16[512,2560]{1,0:T(8,128)(2,1)}, u32[]{:S(2)}, u32[]{:S(2)}) collective-permute-start(bf16[512,2560]{1,0:T(8,128)(2,1)} %bitcast.296), channel_id=1, source_target_pairs={{0,1},{1,0},{2,3},{3,2},{4,5},{5,4},{6,7},{7,6},{8,9},{9,8},{10,11... | collective-permute-start | bytes 7864328 | tf_op jit(solution)/shard_map/ppermute | solution.py:105
  8.6 316.7 %copy-start.66 = (f32[2560]{0:T(1024)}, f32[2560]{0:T(1024)S(1)}, u32[]{:S(2)}) copy-start(f32[2560]{0:T(1024)S(1)} %mul.590) | copy-start | bytes 30724
  11.7 40.0 %copy-start.58 = (f32[2560]{0:T(1024)}, f32[2560]{0:T(1024)S(1)}, u32[]{:S(2)}) copy-start(f32[2560]{0:T(1024)S(1)} %get-tuple-element.338) | copy-start | bytes 30724
  11.8 40.0 %copy-start.60 = (f32[2560]{0:T(1024)}, f32[2560]{0:T(1024)S(1)}, u32[]{:S(2)}) copy-start(f32[2560]{0:T(1024)S(1)} %get-tuple-element.339) | copy-start | bytes 30724
  11.8 40.0 %copy-start.62 = (f32[2560]{0:T(1024)}, f32[2560]{0:T(1024)S(1)}, u32[]{:S(2)}) copy-start(f32[2560]{0:T(1024)S(1)} %get-tuple-element.340) | copy-start | bytes 30724
  11.8 40.0 %copy-start.64 = (f32[2560]{0:T(1024)}, f32[2560]{0:T(1024)S(1)}, u32[]{:S(2)}) copy-start(f32[2560]{0:T(1024)S(1)} %get-tuple-element.341) | copy-start | bytes 30724
  13.3 84.7 %copy-start.80 = (f32[1,256]{1,0:T(1,128)}, f32[1,256]{1,0:T(1,128)S(1)}, u32[]{:S(2)}) copy-start(f32[1,256]{1,0:T(1,128)S(1)} %get-tuple-element.414) | copy-start | bytes 3076
  13.3 84.7 %copy-start.82 = (f32[1,256]{1,0:T(1,128)}, f32[1,256]{1,0:T(1,128)S(1)}, u32[]{:S(2)}) copy-start(f32[1,256]{1,0:T(1,128)S(1)} %get-tuple-element.415) | copy-start | bytes 3076
  13.3 84.7 %copy-start.84 = (f32[1,256]{1,0:T(1,128)}, f32[1,256]{1,0:T(1,128)S(1)}, u32[]{:S(2)}) copy-start(f32[1,256]{1,0:T(1,128)S(1)} %get-tuple-element.416) | copy-start | bytes 3076
  13.3 84.7 %copy-start.86 = (f32[1,256]{1,0:T(1,128)}, f32[1,256]{1,0:T(1,128)S(1)}, u32[]{:S(2)}) copy-start(f32[1,256]{1,0:T(1,128)S(1)} %get-tuple-element.417) | copy-start | bytes 3076
  28.8 22.9 %copy-start.23 = (f32[1024,40]{0,1:T(8,128)}, f32[1024,40]{0,1:T(8,128)S(1)}, u32[]{:S(2)}) copy-start(f32[1024,40]{0,1:T(8,128)S(1)} %get-tuple-element.418) | copy-start | bytes 491524
  32.6 67.2 %copy-start.37 = (f32[4,256,40]{1,2,0:T(8,128)}, f32[4,256,40]{1,2,0:T(8,128)S(1)}, u32[]{:S(2)}) copy-start(f32[4,256,40]{1,2,0:T(8,128)S(1)} %get-tuple-element.413) | copy-start | bytes 491524
  32.6 106.5 %copy-start.42 = (f32[4,256,40]{1,2,0:T(8,128)}, f32[4,256,40]{1,2,0:T(8,128)S(1)}, u32[]{:S(2)}) copy-start(f32[4,256,40]{1,2,0:T(8,128)S(1)} %get-tuple-element.412) | copy-start | bytes 491524
  99.8 38.3 %copy-start.10 = (f32[1024,128]{1,0:T(8,128)}, f32[1024,128]{1,0:T(8,128)S(1)}, u32[]{:S(2)}) copy-start(f32[1024,128]{1,0:T(8,128)S(1)} %get-tuple-element.407) | copy-start | bytes 1572868
  225.4 27.7 %copy-start.21 = (bf16[512,1,2560]{2,0,1:T(8,128)(2,1)S(1)}, bf16[512,1,2560]{2,0,1:T(8,128)(2,1)}, u32[]{:S(2)}) copy-start(bf16[512,1,2560]{2,0,1:T(8,128)(2,1)} %param.37) | copy-start | bytes 7864324
  253.0 46.2 %collective-permute-start.1 = (f32[1024,1]{0,1:T(1,128)S(1)}, f32[1024,1]{0,1:T(1,128)S(1)}, u32[]{:S(2)}, u32[]{:S(2)}) collective-permute-start(f32[1024,1]{0,1:T(1,128)S(1)} %bitcast.343), channel_id=1, source_target_pairs={{0,1},{1,0},{2,3},{3,2},{4,5},{5,4},{6,7},{7,6},{8,9},{9,8},{10,11... | collective-permute-start | bytes 12296 | tf_op jit(solution)/shard_map/ppermute | solution.py:105
  299.2 25.4 %copy-start.76 = (f32[512]{0:T(512)}, f32[512]{0:T(512)S(1)}, u32[]{:S(2)}) copy-start(f32[512]{0:T(512)S(1)} %dynamic-slice.3) | copy-start | bytes 6148
  324.1 1.3 collective-permute-start.4
  465.7 77.6 %slice-start = ((s8[10485760]{0:T(1024)(128)(4,1)}), s8[2097152]{0:T(1024)(128)(4,1)S(1)}, s32[]{:S(2)}) async-start(s8[10485760]{0:T(1024)(128)(4,1)} %bitcast.267), calls=%async_computation.1 | async-start | bytes 4194304
  476.9 66.4 %slice-start.1 = ((s8[10485760]{0:T(1024)(128)(4,1)}), s8[4194304]{0:T(1024)(128)(4,1)S(1)}, s32[]{:S(2)}) async-start(s8[10485760]{0:T(1024)(128)(4,1)} %bitcast.267), calls=%async_computation.2 | async-start | bytes 8388608
  476.9 66.4 %slice-start.2 = ((s8[10485760]{0:T(1024)(128)(4,1)}), s8[4194304]{0:T(1024)(128)(4,1)S(1)}, s32[]{:S(2)}) async-start(s8[10485760]{0:T(1024)(128)(4,1)} %bitcast.267), calls=%async_computation.3 | async-start | bytes 8388608
  476.9 66.4 %copy-start.17 = (f32[4,256,40,64]{1,3,2,0:T(8,128)S(1)}, f32[4,256,40,64]{1,3,2,0:T(8,128)}, u32[]{:S(2)}) copy-start(f32[4,256,40,64]{1,3,2,0:T(8,128)} %get-tuple-element.423) | copy-start | bytes 31457284
  476.9 66.4 %copy-start.39 = (f32[4,256,40]{1,2,0:T(8,128)S(1)}, f32[4,256,40]{1,2,0:T(8,128)}, u32[]{:S(2)}) copy-start(f32[4,256,40]{1,2,0:T(8,128)} %copy-done.37) | copy-start | bytes 491524
  477.0 66.4 %copy-start.45 = (f32[4,256,256]{2,1,0:T(8,128)S(1)}, f32[4,256,256]{2,1,0:T(8,128)}, u32[]{:S(2)}) copy-start(f32[4,256,256]{2,1,0:T(8,128)} %copy-done.44) | copy-start | bytes 3145732
  477.0 66.4 %copy-start.53 = (f32[4,40,256]{2,1,0:T(8,128)S(1)}, f32[4,40,256]{2,1,0:T(8,128)}, u32[]{:S(2)}) copy-start(f32[4,40,256]{2,1,0:T(8,128)} %get-tuple-element.410) | copy-start | bytes 491524
  477.0 66.4 %copy-start.55 = (f32[4,40,256]{2,1,0:T(8,128)S(1)}, f32[4,40,256]{2,1,0:T(8,128)}, u32[]{:S(2)}) copy-start(f32[4,40,256]{2,1,0:T(8,128)} %copy-done.54) | copy-start | bytes 491524
  614.4 25.4 %copy-start.59 = (f32[2560]{0:T(1024)S(1)}, f32[2560]{0:T(1024)}, u32[]{:S(2)}) copy-start(f32[2560]{0:T(1024)} %copy-done.58) | copy-start | bytes 30724
  614.4 25.4 %copy-start.61 = (f32[2560]{0:T(1024)S(1)}, f32[2560]{0:T(1024)}, u32[]{:S(2)}) copy-start(f32[2560]{0:T(1024)} %copy-done.60) | copy-start | bytes 30724
  614.4 25.4 %copy-start.63 = (f32[2560]{0:T(1024)S(1)}, f32[2560]{0:T(1024)}, u32[]{:S(2)}) copy-start(f32[2560]{0:T(1024)} %copy-done.62) | copy-start | bytes 30724
  614.4 25.4 %copy-start.65 = (f32[2560]{0:T(1024)S(1)}, f32[2560]{0:T(1024)}, u32[]{:S(2)}) copy-start(f32[2560]{0:T(1024)} %copy-done.64) | copy-start | bytes 30724
  760.7 278.7 %collective-permute-start.20 = (bf16[1280,2560]{1,0:T(8,128)(2,1)}, bf16[1280,2560]{1,0:T(8,128)(2,1)}, u32[]{:S(2)}, u32[]{:S(2)}) collective-permute-start(bf16[1280,2560]{1,0:T(8,128)(2,1)} %fusion.136), channel_id=1, source_target_pairs={{0,2},{1,5},{2,0},{3,7},{4,6},{5,1},{6,4},{7,3},{8,10},{9,13},{10,... | collective-permute-start | bytes 19660808 | tf_op jit(solution)/shard_map/ppermute | solution.py:118
  774.5 12.9 collective-permute-start.5
  775.7 272.6 %collective-permute-start.11 = (bf16[1280,2560]{1,0:T(8,128)(2,1)}, bf16[1280,2560]{1,0:T(8,128)(2,1)}, u32[]{:S(2)}, u32[]{:S(2)}) collective-permute-start(bf16[1280,2560]{1,0:T(8,128)(2,1)} %fusion.134), channel_id=1, source_target_pairs={{0,2},{1,5},{2,0},{3,7},{4,6},{5,1},{6,4},{7,3},{8,10},{9,13},{10,... | collective-permute-start | bytes 19660808 | tf_op jit(solution)/shard_map/ppermute | solution.py:118
  791.6 117.9 %collective-permute-start.15 = (bf16[1280,168]{0,1:T(8,128)(2,1)S(1)}, bf16[1280,168]{0,1:T(8,128)(2,1)S(1)}, u32[]{:S(2)}, u32[]{:S(2)}) collective-permute-start(bf16[1280,168]{0,1:T(8,128)(2,1)S(1)} %fusion.79), channel_id=1, source_target_pairs={{0,2},{1,5},{2,0},{3,7},{4,6},{5,1},{6,4},{7,3},{8,10},{9,13},{10,... | collective-permute-start | bytes 1290248 | tf_op jit(solution)/shard_map/ppermute | solution.py:118
  809.7 101.6 %copy-start.95 = (f32[40]{0:T(128)S(1)}, f32[40]{0:T(128)}, u32[]{:S(2)}) copy-start(f32[40]{0:T(128)} %param.33) | copy-start | bytes 484
  809.7 109.4 %copy-start.72 = (f32[2560]{0:T(1024)S(1)}, f32[2560]{0:T(1024)}, u32[]{:S(2)}) copy-start(f32[2560]{0:T(1024)} %get-tuple-element.376) | copy-start | bytes 30724
  809.7 135.0 %collective-permute-start.6 = (f32[512,2560]{1,0:T(8,128)}, f32[512,2560]{1,0:T(8,128)}, u32[]{:S(2)}, u32[]{:S(2)}) collective-permute-start(f32[512,2560]{1,0:T(8,128)} %add_add_fusion), channel_id=1, source_target_pairs={{0,1},{1,0},{2,3},{3,2},{4,5},{5,4},{6,7},{7,6},{8,9},{9,8},{10,11... | collective-permute-start | bytes 15728648 | tf_op jit(solution)/shard_map/ppermute | solution.py:105
  809.7 120.4 %collective-permute-start.2 = (bf16[512,2560]{1,0:T(8,128)(2,1)}, bf16[512,2560]{1,0:T(8,128)(2,1)}, u32[]{:S(2)}, u32[]{:S(2)}) collective-permute-start(bf16[512,2560]{1,0:T(8,128)(2,1)} %fusion.65), channel_id=1, source_target_pairs={{0,1},{1,0},{2,3},{3,2},{4,5},{5,4},{6,7},{7,6},{8,9},{9,8},{10,11... | collective-permute-start | bytes 7864328 | tf_op jit(solution)/shard_map/ppermute | solution.py:105
  909.6 5.9 collective-permute-start.16
  915.7 6.8 collective-permute-start.17
  922.7 4.6 collective-permute-start.18
  927.3 1.4 collective-permute-start.19
  928.7 138.5 %collective-permute-start.7 = (bf16[1280,2560]{1,0:T(8,128)(2,1)}, bf16[1280,2560]{1,0:T(8,128)(2,1)}, u32[]{:S(2)}, u32[]{:S(2)}) collective-permute-start(bf16[1280,2560]{1,0:T(8,128)(2,1)} %fusion.132), channel_id=1, source_target_pairs={{0,2},{1,5},{2,0},{3,7},{4,6},{5,1},{6,4},{7,3},{8,10},{9,13},{10,... | collective-permute-start | bytes 19660808 | tf_op jit(solution)/shard_map/ppermute | solution.py:118
  1047.3 41.7 %collective-permute-start.21 = (bf16[640,2560]{1,0:T(8,128)(2,1)S(1)}, bf16[640,2560]{1,0:T(8,128)(2,1)}, u32[]{:S(2)}, u32[]{:S(2)}) collective-permute-start(bf16[640,2560]{1,0:T(8,128)(2,1)S(1)} %slice.339), channel_id=1, source_target_pairs={{0,4},{1,3},{2,6},{3,1},{4,0},{5,7},{6,2},{7,5},{8,12},{9,11},{10,... | collective-permute-start | bytes 9830408 | tf_op jit(solution)/shard_map/ppermute | solution.py:112
  1061.0 25.0 %slice-start.15 = ((s8[5242880]{0:T(1024)(128)(4,1)}), s8[4194304]{0:T(1024)(128)(4,1)S(1)}, s32[]{:S(2)}) async-start(s8[5242880]{0:T(1024)(128)(4,1)} %bitcast.308), calls=%async_computation.16 | async-start | bytes 8388608
  1066.1 55.2 %collective-permute-start.12 = (bf16[640,2560]{1,0:T(8,128)(2,1)}, bf16[640,2560]{1,0:T(8,128)(2,1)}, u32[]{:S(2)}, u32[]{:S(2)}) collective-permute-start(bf16[640,2560]{1,0:T(8,128)(2,1)} %slice.340), channel_id=1, source_target_pairs={{0,4},{1,3},{2,6},{3,1},{4,0},{5,7},{6,2},{7,5},{8,12},{9,11},{10,... | collective-permute-start | bytes 9830408 | tf_op jit(solution)/shard_map/ppermute | solution.py:112
  1085.0 71.4 %collective-permute-start.8 = (bf16[640,2560]{1,0:T(8,128)(2,1)}, bf16[640,2560]{1,0:T(8,128)(2,1)}, u32[]{:S(2)}, u32[]{:S(2)}) collective-permute-start(bf16[640,2560]{1,0:T(8,128)(2,1)} %slice.341), channel_id=1, source_target_pairs={{0,4},{1,3},{2,6},{3,1},{4,0},{5,7},{6,2},{7,5},{8,12},{9,11},{10,... | collective-permute-start | bytes 9830408 | tf_op jit(solution)/shard_map/ppermute | solution.py:112
  1089.0 67.4 %slice-start.3 = ((s8[13107200]{0:T(1024)(128)(4,1)}), s8[524288]{0:T(1024)(128)(4,1)S(1)}, s32[]{:S(2)}) async-start(s8[13107200]{0:T(1024)(128)(4,1)} %bitcast.271), calls=%async_computation.4 | async-start | bytes 1048576
  1089.0 67.4 %slice-start.4 = ((s8[13107200]{0:T(1024)(128)(4,1)}), s8[4194304]{0:T(1024)(128)(4,1)S(1)}, s32[]{:S(2)}) async-start(s8[13107200]{0:T(1024)(128)(4,1)} %bitcast.271), calls=%async_computation.5 | async-start | bytes 8388608
  1097.0 59.4 %slice-start.5 = ((s8[13107200]{0:T(1024)(128)(4,1)}), s8[4194304]{0:T(1024)(128)(4,1)S(1)}, s32[]{:S(2)}) async-start(s8[13107200]{0:T(1024)(128)(4,1)} %bitcast.271), calls=%async_computation.6 | async-start | bytes 8388608
  1097.0 59.4 %slice-start.6 = ((s8[13107200]{0:T(1024)(128)(4,1)}), s8[4194304]{0:T(1024)(128)(4,1)S(1)}, s32[]{:S(2)}) async-start(s8[13107200]{0:T(1024)(128)(4,1)} %bitcast.271), calls=%async_computation.7 | async-start | bytes 8388608
  1097.0 139.9 %collective-permute-start.22 = (bf16[320,2560]{1,0:T(8,128)(2,1)S(1)}, bf16[320,2560]{1,0:T(8,128)(2,1)S(1)}, u32[]{:S(2)}, u32[]{:S(2)}) collective-permute-start(bf16[320,2560]{1,0:T(8,128)(2,1)S(1)} %slice.342), channel_id=1, source_target_pairs={{0,16},{1,17},{2,18},{3,19},{4,20},{5,21},{6,22},{7,23},{8,24},{9,... | collective-permute-start | bytes 4915208 | tf_op jit(solution)/shard_map/ppermute | solution.py:112
  1130.8 141.2 %collective-permute-start.13 = (bf16[320,2560]{1,0:T(8,128)(2,1)S(1)}, bf16[320,2560]{1,0:T(8,128)(2,1)S(1)}, u32[]{:S(2)}, u32[]{:S(2)}) collective-permute-start(bf16[320,2560]{1,0:T(8,128)(2,1)S(1)} %slice.343), channel_id=1, source_target_pairs={{0,16},{1,17},{2,18},{3,19},{4,20},{5,21},{6,22},{7,23},{8,24},{9,... | collective-permute-start | bytes 4915208 | tf_op jit(solution)/shard_map/ppermute | solution.py:112
  1162.1 109.9 %slice-start.7 = ((s8[6553600]{0:T(1024)(128)(4,1)}), s8[4194304]{0:T(1024)(128)(4,1)S(1)}, s32[]{:S(2)}) async-start(s8[6553600]{0:T(1024)(128)(4,1)} %bitcast.278), calls=%async_computation.8 | async-start | bytes 8388608
  1164.4 107.6 %slice-start.8 = ((s8[6553600]{0:T(1024)(128)(4,1)}), s8[2359296]{0:T(1024)(128)(4,1)S(1)}, s32[]{:S(2)}) async-start(s8[6553600]{0:T(1024)(128)(4,1)} %bitcast.278), calls=%async_computation.9 | async-start | bytes 4718592
  1164.4 142.4 %collective-permute-start.9 = (bf16[320,2560]{1,0:T(8,128)(2,1)S(1)}, bf16[320,2560]{1,0:T(8,128)(2,1)S(1)}, u32[]{:S(2)}, u32[]{:S(2)}) collective-permute-start(bf16[320,2560]{1,0:T(8,128)(2,1)S(1)} %slice.344), channel_id=1, source_target_pairs={{0,16},{1,17},{2,18},{3,19},{4,20},{5,21},{6,22},{7,23},{8,24},{9,... | collective-permute-start | bytes 4915208 | tf_op jit(solution)/shard_map/ppermute | solution.py:112
  1236.9 69.9 %slice-start.9 = ((s8[6553600]{0:T(1024)(128)(4,1)}), s8[4194304]{0:T(1024)(128)(4,1)S(1)}, s32[]{:S(2)}) async-start(s8[6553600]{0:T(1024)(128)(4,1)} %bitcast.280), calls=%async_computation.10 | async-start | bytes 8388608
  1239.5 67.3 %slice-start.10 = ((s8[6553600]{0:T(1024)(128)(4,1)}), s8[2359296]{0:T(1024)(128)(4,1)S(1)}, s32[]{:S(2)}) async-start(s8[6553600]{0:T(1024)(128)(4,1)} %bitcast.280), calls=%async_computation.11 | async-start | bytes 4718592
  1239.5 85.9 %collective-permute-start.23 = (bf16[160,2560]{1,0:T(8,128)(2,1)S(1)}, bf16[160,2560]{1,0:T(8,128)(2,1)S(1)}, u32[]{:S(2)}, u32[]{:S(2)}) collective-permute-start(bf16[160,2560]{1,0:T(8,128)(2,1)S(1)} %slice.345), channel_id=1, source_target_pairs={{0,8},{1,9},{2,10},{3,11},{4,12},{5,13},{6,14},{7,15},{8,0},{9,1},... | collective-permute-start | bytes 2457608 | tf_op jit(solution)/shard_map/ppermute | solution.py:112
  1272.5 70.4 %collective-permute-start.14 = (bf16[160,2560]{1,0:T(8,128)(2,1)S(1)}, bf16[160,2560]{1,0:T(8,128)(2,1)S(1)}, u32[]{:S(2)}, u32[]{:S(2)}) collective-permute-start(bf16[160,2560]{1,0:T(8,128)(2,1)S(1)} %slice.346), channel_id=1, source_target_pairs={{0,8},{1,9},{2,10},{3,11},{4,12},{5,13},{6,14},{7,15},{8,0},{9,1},... | collective-permute-start | bytes 2457608 | tf_op jit(solution)/shard_map/ppermute | solution.py:112
  1307.3 53.1 %collective-permute-start.10 = (bf16[160,2560]{1,0:T(8,128)(2,1)S(1)}, bf16[160,2560]{1,0:T(8,128)(2,1)S(1)}, u32[]{:S(2)}, u32[]{:S(2)}) collective-permute-start(bf16[160,2560]{1,0:T(8,128)(2,1)S(1)} %slice.347), channel_id=1, source_target_pairs={{0,8},{1,9},{2,10},{3,11},{4,12},{5,13},{6,14},{7,15},{8,0},{9,1},... | collective-permute-start | bytes 2457608 | tf_op jit(solution)/shard_map/ppermute | solution.py:112
  (76 other events, 947.9 us)
Sparse Core Ops, SparseCore 0:
  928.2 107.2 all-reduce.22
